TPU v7x, 256 devices: a whole 4x4x8 slice. The times are simulated.
256 devices in a mesh: section: 32 (over x_hi, z, core), expert: 8 (over x_lo, y).
Axes of the slice: x: 4 (x_hi: 2, x_lo: 2; x = x_hi * 2 + x_lo), y: 4, z: 8, core: 2. Of those that a mesh axis runs over, the one named last changes fastest.
Arguments:
- tokens: bfloat16 [1536, 6144], P('expert', 'section'), may hold values from -6 to 6
- expert_ids: int32 [1536, 2], P('expert'), may hold values from 0 to 7, as said below
- slot_ids: int32 [1536, 2], P('expert'), may hold values from 0 to 47, as said below
- router: float32 [6144, 8], replicated, may hold values from -0.078125 to 0.078125
- up_weight: bfloat16 [8, 6144, 8192], P('expert', None, 'section'), may hold values from -0.078125 to 0.078125
- down_weight: bfloat16 [8, 8192, 6144], P('expert', 'section'), may hold values from -0.0625 to 0.0625
- cotangent: bfloat16 [1536, 6144], P('expert', 'section'), may hold values from -6 to 6
Outputs:
- mixed: bfloat16 [1536, 6144], P('expert', 'section')
- grad_tokens: bfloat16 [1536, 6144], P('expert', 'section')
- grad_up: bfloat16 [8, 6144, 8192], P('expert', None, 'section')
- grad_down: bfloat16 [8, 8192, 6144], P('expert', 'section')
- grad_router: float32 [6144, 8], replicated
Inputs may be any that keep to these rules, and one draw needn't show every extreme that they name: `expert_ids`: within each block of 192 consecutive tokens (one group), a token's two experts differ and every expert is chosen exactly 48 times. `slot_ids`: within each block of 192 consecutive tokens, the 48 choices of one expert take the slots 0 to 47 once each.
All inputs are finite; a program needn't handle non-finite values.
Results may differ from a plain program's by a relative error of at most 0.019.
Values may be sent and summed in bfloat16 or wider, within the bound.
A program may use at most 128 MiB of HBM per device.

v0:
```python
import jax
import jax.numpy as jnp
from jax import lax
from jax.sharding import PartitionSpec as P


def gate_values(logits, choose):
    picked = jnp.sum(logits[:, None, :] * choose, axis=2)
    logit_gap = picked[:, 0] - picked[:, 1]
    return jnp.stack([jax.nn.sigmoid(logit_gap), jax.nn.sigmoid(-logit_gap)], axis=1)


def dispatch_rows(slot_place, gate_pair, rows_in, rows_cot, slot_total):
    select = (
        jnp.arange(slot_total, dtype=jnp.int32)[:, None, None] == slot_place[None, :, :]
    ).astype(jnp.float32)
    gate_row = jnp.sum(select * gate_pair[None, :, :], axis=(1, 2))
    picker = jnp.sum(select, axis=2).astype(jnp.bfloat16)
    sent_in = jnp.dot(picker, rows_in, preferred_element_type=jnp.float32).astype(jnp.bfloat16)
    sent_cot = jnp.dot(picker, rows_cot, preferred_element_type=jnp.float32)
    sent_cot = (sent_cot * gate_row[:, None]).astype(jnp.bfloat16)
    return (sent_in, sent_cot)


def shards(tokens, expert_ids, slot_ids, router, up_weight, down_weight, cotangent):
    token_count, feat_slice = tokens.shape
    model_width, n_expert = router.shape
    slot_cap = 2 * token_count // n_expert
    slot_total = n_expert * slot_cap
    feat_start = lax.axis_index("section") * feat_slice
    router_rows = lax.dynamic_slice_in_dim(router, feat_start, feat_slice, 0)
    choose = (
        expert_ids[:, :, None] == jnp.arange(n_expert, dtype=jnp.int32)[None, None, :]
    ).astype(jnp.float32)
    slot_place = expert_ids * slot_cap + slot_ids
    full_in, full_cot = (
        lax.all_gather(tokens, "section", axis=1, tiled=True),
        lax.all_gather(cotangent, "section", axis=1, tiled=True),
    )
    logits = jnp.dot(full_in.astype(jnp.float32), router, precision=lax.Precision.HIGHEST)
    gate_pair = gate_values(logits, choose)
    sent_in, sent_cot = dispatch_rows(slot_place, gate_pair, full_in, full_cot, slot_total)
    block_shape = (n_expert, slot_cap, model_width)
    rows_in, rows_cot = (
        lax.all_to_all(
            sent_in.reshape(block_shape), "expert", split_axis=0, concat_axis=0, tiled=True
        ),
        lax.all_to_all(
            sent_cot.reshape(block_shape), "expert", split_axis=0, concat_axis=0, tiled=True
        ),
    )
    rows_in = rows_in.reshape(slot_total, model_width)
    rows_cot = rows_cot.reshape(slot_total, model_width)
    weight_in = up_weight[0]
    weight_out = down_weight[0]
    pre_act = jnp.dot(rows_in, weight_in, preferred_element_type=jnp.float32)
    sigma = jax.nn.sigmoid(pre_act)
    hidden = (pre_act * sigma).astype(jnp.bfloat16)
    hidden_grad = lax.dot_general(
        rows_cot, weight_out, (((1,), (1,)), ((), ())), preferred_element_type=jnp.float32
    )
    pre_grad = (hidden_grad * sigma * (1.0 + pre_act * (1.0 - sigma))).astype(jnp.bfloat16)
    grad_down = lax.dot_general(
        hidden, rows_cot, (((0,), (0,)), ((), ())), preferred_element_type=jnp.float32
    ).astype(jnp.bfloat16)
    grad_up = lax.dot_general(
        rows_in, pre_grad, (((0,), (0,)), ((), ())), preferred_element_type=jnp.float32
    ).astype(jnp.bfloat16)
    forward_part = jnp.dot(hidden, weight_out, preferred_element_type=jnp.float32)
    backward_part = lax.dot_general(
        pre_grad, weight_in, (((1,), (1,)), ((), ())), preferred_element_type=jnp.float32
    )
    out_sum, back_sum = (
        lax.psum_scatter(
            forward_part.astype(jnp.bfloat16), "section", scatter_dimension=1, tiled=True
        ).astype(jnp.float32),
        lax.psum_scatter(
            backward_part.astype(jnp.bfloat16), "section", scatter_dimension=1, tiled=True
        ).astype(jnp.float32),
    )
    return_shape = (n_expert, slot_cap, feat_slice)
    came_out, came_back = (
        lax.all_to_all(
            out_sum.astype(jnp.bfloat16).reshape(return_shape),
            "expert",
            split_axis=0,
            concat_axis=0,
            tiled=True,
        ),
        lax.all_to_all(
            back_sum.astype(jnp.bfloat16).reshape(return_shape),
            "expert",
            split_axis=0,
            concat_axis=0,
            tiled=True,
        ),
    )
    flat_out = came_out.reshape(slot_total, feat_slice)
    flat_back = came_back.reshape(slot_total, feat_slice)
    positions = jnp.arange(slot_total, dtype=jnp.int32)
    take_first = (slot_place[:, 0:1] == positions[None, :]).astype(jnp.bfloat16)
    take_second = (slot_place[:, 1:2] == positions[None, :]).astype(jnp.bfloat16)
    out_first = jnp.dot(take_first, flat_out, preferred_element_type=jnp.float32)
    out_second = jnp.dot(take_second, flat_out, preferred_element_type=jnp.float32)
    mixed = gate_pair[:, 0:1] * out_first + gate_pair[:, 1:2] * out_second
    cot_float = cotangent.astype(jnp.float32)
    grad_first, grad_second = lax.psum(
        (jnp.sum(cot_float * out_first, axis=1), jnp.sum(cot_float * out_second, axis=1)), "section"
    )
    logit_grad = (grad_first - grad_second) * gate_pair[:, 0] * gate_pair[:, 1]
    logits_grad = (choose[:, 0, :] - choose[:, 1, :]) * logit_grad[:, None]
    back_first = jnp.dot(take_first, flat_back, preferred_element_type=jnp.float32)
    back_second = jnp.dot(take_second, flat_back, preferred_element_type=jnp.float32)
    grad_tokens = (
        back_first
        + back_second
        + jnp.dot(logits_grad, router_rows.T, precision=lax.Precision.HIGHEST)
    )
    local_router = jnp.dot(
        tokens.astype(jnp.float32).T, logits_grad, precision=lax.Precision.HIGHEST
    )
    placed_router = lax.dynamic_update_slice(
        jnp.zeros((model_width, n_expert), jnp.float32), local_router, (feat_start, jnp.int32(0))
    )
    grad_router = lax.psum(placed_router, ("section", "expert"))
    return (
        mixed.astype(jnp.bfloat16),
        grad_tokens.astype(jnp.bfloat16),
        grad_up[None],
        grad_down[None],
        grad_router,
    )


def solution(mesh):
    in_specs = (
        P("expert", "section"),
        P("expert", None),
        P("expert", None),
        P(),
        P("expert", None, "section"),
        P("expert", "section", None),
        P("expert", "section"),
    )
    out_specs = (
        P("expert", "section"),
        P("expert", "section"),
        P("expert", None, "section"),
        P("expert", "section", None),
        P(),
    )
    return jax.shard_map(shards, mesh=mesh, in_specs=in_specs, out_specs=out_specs, check_vma=False)
```

profile of v0, /device:TPU:1, one launch (start us, length us, event | category | flops | bytes accessed | tf_op | source)
XLA Modules:
  0.0 798.1 jit_solution(7832499318834523150)
XLA Ops:
  7.2 0.0 all-gather.3.cloned.1.call-start
  7.2 1.8 copy.35
  9.0 0.7 multiply_add_fusion
  9.7 88.7 %all-gather.3.cloned.1.call-done = bf16[192,6144]{0,1:T(8,128)(2,1)} async-done(((bf16[192,192]{0,1:T(8,128)(2,1)}), bf16[192,6144]{0,1:T(8,128)(2,1)}) %all-gather.3.cloned.1.call-update) | async-done | bytes 2359312 | tf_op jit(solution)/shard_map/all_gather | solution.py:37
  98.5 3.4 fusion.39
  101.8 0.7 select_reduce_fusion.1
  102.6 0.5 copy-done.10
  103.2 0.2 select_reduce_fusion
  103.4 3.7 convolution_convert_fusion.2
  107.0 4.7 all-to-all-start
  111.8 0.0 all-gather.5.cloned.1.call-start
  111.8 0.7 copy.37
  112.6 0.0 reduce-scatter.3.cloned.1.call-start
  112.6 53.5 %all-to-all-done = bf16[8,48,6144]{2,1,0:T(8,128)(2,1)} async-done(((bf16[8,48,6144]{2,1,0:T(8,128)(2,1)}), bf16[8,48,6144]{2,1,0:T(8,128)(2,1)}, u32[]{:S(2)}, u32[]{:S(2)}) %all-to-all-start) | async-done | bytes 4718624 | tf_op jit(solution)/shard_map/all_to_all | solution.py:45
  166.2 4.7 fusion.6
  170.9 4.1 convolution_convert_fusion.1
  175.0 0.0 reduce-scatter.5.cloned.1.call-start
  175.1 21.7 %all-gather.5.cloned.1.call-done = bf16[192,6144]{0,1:T(8,128)(2,1)} async-done(((bf16[192,192]{0,1:T(8,128)(2,1)}), bf16[192,6144]{0,1:T(8,128)(2,1)}) %all-gather.5.cloned.1.call-update) | async-done | bytes 2359312 | tf_op jit(solution)/shard_map/all_gather | solution.py:38
  196.7 3.8 multiply_convert_fusion
  200.6 61.3 %all_to_all.20 = bf16[8,48,6144]{2,1,0:T(8,128)(2,1)S(1)} all-to-all(bf16[8,48,6144]{2,1,0:T(8,128)(2,1)S(1)} %bitcast.60), channel_id=1, replica_groups=mesh['section'=32,'expert'=8] {'expert'}, dimensions={0} | all-to-all | bytes 9437184 | tf_op jit(solution)/shard_map/all_to_all | solution.py:48
  261.9 2.1 copy-done.1
  264.0 1.4 fusion.14
  265.4 0.7 copy-done.6
  266.1 4.0 convolution_convert_fusion
  270.2 0.6 fusion.38
  270.8 0.7 fusion.30
  271.4 5.9 fusion
  277.3 49.2 %reduce-scatter.3.cloned.1.call-done = bf16[384,192]{0,1:T(8,128)(2,1)} async-done(((bf16[384,6144]{0,1:T(8,128)(2,1)}), bf16[384,192]{0,1:T(8,128)(2,1)}) %reduce-scatter.3.cloned.1.call-update) | async-done | bytes 147472 | tf_op jit(solution)/shard_map/reduce_scatter | solution.py:74
  326.5 1.7 copy.36
  328.2 4.9 all-to-all-start.1
  333.1 5.9 fusion.1
  338.9 121.7 %reduce-scatter.5.cloned.1.call-done = bf16[384,192]{0,1:T(8,128)(2,1)} async-done(((bf16[384,6144]{0,1:T(8,128)(2,1)}), bf16[384,192]{0,1:T(8,128)(2,1)}) %reduce-scatter.5.cloned.1.call-update) | async-done | bytes 147472 | tf_op jit(solution)/shard_map/reduce_scatter | solution.py:77
  460.6 1.7 copy.38
  462.3 3.8 all-to-all-start.3
  466.2 1.2 fusion.21
  467.4 2.0 fusion.23
  469.4 70.1 %all-reduce = (f32[192]{0:T(256)S(1)}, f32[192]{0:T(256)S(1)}) all-reduce(f32[192]{0:T(256)S(1)} %get-tuple-element.26, f32[192]{0:T(256)S(1)} %get-tuple-element.25), channel_id=1, replica_groups=mesh['section'=32,'expert'=8] {'section'}, use_global_device_ids=true, to_apply=%region_6.0 | all-reduce | flops 384 | bytes 3072 | tf_op jit(solution)/shard_map/psum | solution.py:107
  539.4 0.7 multiply_multiply_fusion
  540.1 0.6 copy-done.8
  540.7 1.7 convolution_bitcast_fusion
  542.3 0.9 dynamic_update_slice.3
  543.3 0.7 copy-done.5
  544.0 1.1 fusion.33
  545.1 0.9 fusion.20
  546.0 1.6 fusion.18
  547.6 1.6 copy.40
  549.2 240.7 %all-reduce.3.cloned.1.call-done = f32[6144,8]{0,1:T(8,128)} async-done(((f32[6144,8]{0,1:T(8,128)}), f32[6144,8]{0,1:T(8,128)}) %all-reduce.3.cloned.1.call-update) | async-done | bytes 196624 | tf_op jit(solution)/shard_map/psum | solution.py:125
  789.9 1.6 copy.43
  (29 shorter events, 0.2 us)
Async XLA Ops:
  7.2 163.7 %copy-start = (bf16[1,256,6144]{2,1,0:T(8,128)(2,1)S(1)}, bf16[1,256,6144]{2,1,0:T(8,128)(2,1)}, u32[]{:S(2)}) copy-start(bf16[1,256,6144]{2,1,0:T(8,128)(2,1)} %param.12) | copy-start | bytes 9437188
  7.2 91.3 %all-gather.3.cloned.1.call-start = ((), (), s32[]{:S(2)}) async-start(), calls=%async_computation.6 | async-start | bytes 3244032 | tf_op jit(solution)/shard_map/all_gather | solution.py:37
  98.5 4.9 copy-start.2
  102.6 0.6 copy-start.10
  102.6 0.6 copy-start.9
  103.3 3.7 copy-start.4
  107.0 4.8 copy-start.7
  107.0 59.1 %all-to-all-start = ((bf16[8,48,6144]{2,1,0:T(8,128)(2,1)}), bf16[8,48,6144]{2,1,0:T(8,128)(2,1)}, u32[]{:S(2)}, u32[]{:S(2)}) async-start(bf16[8,48,6144]{2,1,0:T(8,128)(2,1)} %bitcast.59), calls=%async_computation | async-start | bytes 9437184 | tf_op jit(solution)/shard_map/all_to_all | solution.py:45
  111.8 85.0 %all-gather.5.cloned.1.call-start = ((), (), s32[]{:S(2)}) async-start(), calls=%async_computation.8 | async-start | bytes 3244032 | tf_op jit(solution)/shard_map/all_gather | solution.py:38
  112.6 213.9 %reduce-scatter.3.cloned.1.call-start = ((), (), s32[]{:S(2)}) async-start(), calls=%async_computation.7 | async-start | bytes 4866048 | tf_op jit(solution)/shard_map/reduce_scatter | solution.py:74
  175.0 285.6 %reduce-scatter.5.cloned.1.call-start = ((), (), s32[]{:S(2)}) async-start(), calls=%async_computation.9 | async-start | bytes 4866048 | tf_op jit(solution)/shard_map/reduce_scatter | solution.py:77
  261.9 2.1 copy-start.1
  264.0 2.1 copy-start.3
  265.4 0.7 copy-start.6
  328.2 134.1 %all-to-all-start.1 = ((bf16[8,48,192]{2,1,0:T(8,128)(2,1)}), bf16[8,48,192]{2,1,0:T(8,128)(2,1)}, u32[]{:S(2)}, u32[]{:S(2)}) async-start(bf16[8,48,192]{2,1,0:T(8,128)(2,1)} %bitcast.63), calls=%async_computation.2 | async-start | bytes 393216 | tf_op jit(solution)/shard_map/all_to_all | solution.py:83
  462.3 82.7 %all-to-all-start.3 = ((bf16[8,48,192]{2,1,0:T(8,128)(2,1)}), bf16[8,48,192]{2,1,0:T(8,128)(2,1)S(1)}, u32[]{:S(2)}, u32[]{:S(2)}) async-start(bf16[8,48,192]{2,1,0:T(8,128)(2,1)} %bitcast.12), calls=%async_computation.5 | async-start | bytes 393216 | tf_op jit(solution)/shard_map/all_to_all | solution.py:90
  466.1 323.8 %all-reduce.3.cloned.1.call-start = ((), (), s32[]{:S(2)}) async-start(), calls=%async_computation.10 | async-start | bytes 393216 | tf_op jit(solution)/shard_map/psum | solution.py:125
  540.1 0.6 copy-start.8
  543.3 0.7 copy-start.5
Sparse Core Ops, SparseCore 0:
  11.3 87.0 all-gather.2
  115.9 80.7 all-gather.4
  201.0 125.4 reduce-scatter.2
  330.6 129.9 reduce-scatter.4
  544.1 245.8 all-reduce.2
where the time goes:
time: 799 us; the launch traced here: 798 us
  waiting for transfers between devices  576 us (72%)
  blocking collectives  131 us (16%)
  matrix products  45.3 us (6%)
  local copies, waits for them, and re-layouts  15.4 us (2%)
  between operations  14 us (2%)
  starting transfers between devices  13.5 us (2%)
    psum x1, waiting for transfers between devices, shards(): grad_router = lax.psum(placed_router, ('section', 'expert'))  241 us
    reduce_scatter x1, waiting for transfers between devices, shards(): lax.psum_scatter(backward_part.astype(jnp.bfloat16), 'section', scatter_d...  122 us
    all_gather x1, waiting for transfers between devices, shards(): lax.all_gather(tokens, 'section', axis=1, tiled=True)  88.7 us
    psum x1, blocking collectives, shards(): lax.psum((jnp.sum(cot_float * out_first, axis=1), jnp.sum(cot_float * out...  70.1 us
    all_to_all x1, blocking collectives, shards(): lax.all_to_all(sent_cot.reshape(block_shape), 'expert', split_axis=0, con...  61.3 us
    all_to_all x1, waiting for transfers between devices, shards(): lax.all_to_all(sent_in.reshape(block_shape), 'expert', split_axis=0, conc...  53.5 us
    reduce_scatter x1, waiting for transfers between devices, shards(): lax.psum_scatter(forward_part.astype(jnp.bfloat16), 'section', scatter_di...  49.2 us
    all_gather x1, waiting for transfers between devices, shards(): lax.all_gather(cotangent, 'section', axis=1, tiled=True)  21.7 us
  transfers between devices with their start and end apart: 8, of which 6 were waited for; matrix products, arithmetic and copies ran while one was open for 6% of the time, Pallas kernels for 0%

commit v1 on v0

--- a/solution.py
+++ b/solution.py
@@ -122,7 +122,7 @@
     placed_router = lax.dynamic_update_slice(
         jnp.zeros((model_width, n_expert), jnp.float32), local_router, (feat_start, jnp.int32(0))
     )
-    grad_router = lax.psum(placed_router, ("section", "expert"))
+    grad_router = jnp.sum(lax.all_gather(placed_router, ("section", "expert")), axis=0)
     return (
         mixed.astype(jnp.bfloat16),
         grad_tokens.astype(jnp.bfloat16),

time: 799 us -> 1270 us (1.59)
  waiting for transfers between devices: 576 us -> 1030 us
  other arithmetic: 2.99 us -> 20 us
    all_gather x0 -> x1, waiting for transfers between devices: none -> 763 us  [shards(): lax.all_gather(placed_router, ('section', 'expert'))]
    psum x1 -> x0, waiting for transfers between devices: 241 us -> none  [shards(): grad_router = lax.psum(placed_router, ('section', 'expert'))]
    reduce_scatter x1, waiting for transfers between devices: 122 us -> 35.8 us  [shards(): lax.psum_scatter(backward_part.astype(jnp.bfloat16), 'section', scatter_d...]
    reduce_sum x0 -> x1, other arithmetic: none -> 18.4 us  [shards(): jnp.sum(lax.all_gather(placed_router, ('section', 'expert')), axis=0)]
  transfers between devices with their start and end apart: 8 -> 8, of which waited for: 6 -> 8; matrix products, arithmetic and copies ran while one was open for 6% -> 3% of each run, Pallas kernels for 0% -> 0%
where the time goes in v1:
time: 1270 us; the launch traced here: 1260 us
  waiting for transfers between devices  1030 us (81%)
  blocking collectives  133 us (10%)
  matrix products  39.8 us (3%)
  other arithmetic  20 us (2%)
  starting transfers between devices  14.7 us (1%)
  between operations  14 us (1%)
    all_gather x1, waiting for transfers between devices, shards(): lax.all_gather(placed_router, ('section', 'expert'))  763 us
    all_gather x1, waiting for transfers between devices, shards(): lax.all_gather(tokens, 'section', axis=1, tiled=True)  88.7 us
    psum x1, blocking collectives, shards(): lax.psum((jnp.sum(cot_float * out_first, axis=1), jnp.sum(cot_float * out...  71.3 us
    all_to_all x1, blocking collectives, shards(): lax.all_to_all(sent_cot.reshape(block_shape), 'expert', split_axis=0, con...  61.3 us
    reduce_scatter x1, waiting for transfers between devices, shards(): lax.psum_scatter(forward_part.astype(jnp.bfloat16), 'section', scatter_di...  56.3 us
    all_to_all x1, waiting for transfers between devices, shards(): lax.all_to_all(sent_in.reshape(block_shape), 'expert', split_axis=0, conc...  53.5 us
    reduce_scatter x1, waiting for transfers between devices, shards(): lax.psum_scatter(backward_part.astype(jnp.bfloat16), 'section', scatter_d...  35.8 us
  transfers between devices with their start and end apart: 8, of which 8 were waited for; matrix products, arithmetic and copies ran while one was open for 3% of the time, Pallas kernels for 0%

profile of v1, /device:TPU:1, one launch (start us, length us, event | category | flops | bytes accessed | tf_op | source)
XLA Modules:
  0.0 1260.7 jit_solution(17843219032132230114)
XLA Ops:
  7.2 0.0 all-gather.4.cloned.1.call-start
  7.2 1.8 copy.35
  9.0 0.0 all-gather.4.cloned.1.call-update
  9.0 0.7 multiply_add_fusion
  9.7 88.7 %all-gather.4.cloned.1.call-done = bf16[192,6144]{0,1:T(8,128)(2,1)} async-done(((bf16[192,192]{0,1:T(8,128)(2,1)}), bf16[192,6144]{0,1:T(8,128)(2,1)}) %all-gather.4.cloned.1.call-update) | async-done | bytes 2359312 | tf_op jit(solution)/shard_map/all_gather | solution.py:37
  98.5 3.4 fusion.39
  101.8 0.7 select_reduce_fusion.1
  102.6 0.2 select_reduce_fusion
  102.8 3.6 convolution_convert_fusion.2
  106.4 4.7 all-to-all-start
  111.2 0.0 all-gather.6.cloned.1.call-start
  111.2 0.7 copy.37
  112.0 0.0 reduce-scatter.3.cloned.1.call-start
  112.0 53.5 %all-to-all-done = bf16[8,48,6144]{2,1,0:T(8,128)(2,1)} async-done(((bf16[8,48,6144]{2,1,0:T(8,128)(2,1)}), bf16[8,48,6144]{2,1,0:T(8,128)(2,1)}, u32[]{:S(2)}, u32[]{:S(2)}) %all-to-all-start) | async-done | bytes 4718624 | tf_op jit(solution)/shard_map/all_to_all | solution.py:45
  165.6 4.7 fusion.6
  170.3 4.0 convolution_convert_fusion.1
  174.4 0.0 reduce-scatter.5.cloned.1.call-start
  174.4 21.7 %all-gather.6.cloned.1.call-done = bf16[192,6144]{0,1:T(8,128)(2,1)} async-done(((bf16[192,192]{0,1:T(8,128)(2,1)}), bf16[192,6144]{0,1:T(8,128)(2,1)}) %all-gather.6.cloned.1.call-update) | async-done | bytes 2359312 | tf_op jit(solution)/shard_map/all_gather | solution.py:38
  196.1 3.8 multiply_convert_fusion
  200.0 61.3 %all_to_all.20 = bf16[8,48,6144]{2,1,0:T(8,128)(2,1)S(1)} all-to-all(bf16[8,48,6144]{2,1,0:T(8,128)(2,1)S(1)} %bitcast.62), channel_id=1, replica_groups=mesh['section'=32,'expert'=8] {'expert'}, dimensions={0} | all-to-all | bytes 9437184 | tf_op jit(solution)/shard_map/all_to_all | solution.py:48
  261.2 2.2 copy-done.2
  263.5 1.4 fusion.14
  264.9 0.7 copy-done.9
  265.6 4.0 convolution_convert_fusion
  269.6 56.3 %reduce-scatter.3.cloned.1.call-done = bf16[384,192]{0,1:T(8,128)(2,1)} async-done(((bf16[384,6144]{0,1:T(8,128)(2,1)}), bf16[384,192]{0,1:T(8,128)(2,1)}) %reduce-scatter.3.cloned.1.call-update) | async-done | bytes 147472 | tf_op jit(solution)/shard_map/reduce_scatter | solution.py:74
  325.9 1.7 copy.36
  327.6 4.9 all-to-all-start.1
  332.5 0.0 all-gather.8.cloned.1.call-start
  332.5 5.7 all-to-all-done.1
  338.3 0.3 fusion.21
  338.6 0.3 fusion.23
  338.9 71.3 %all-reduce = (f32[192]{0:T(256)S(1)}, f32[192]{0:T(256)S(1)}) all-reduce(f32[192]{0:T(256)S(1)} %get-tuple-element.26, f32[192]{0:T(256)S(1)} %get-tuple-element.25), channel_id=1, replica_groups=mesh['section'=32,'expert'=8] {'section'}, use_global_device_ids=true, to_apply=%region_6.0 | all-reduce | flops 384 | bytes 3072 | tf_op jit(solution)/shard_map/psum | solution.py:107
  410.2 0.1 convolution_bitcast_fusion
  410.3 0.1 broadcast_in_dim.8
  410.4 0.3 dynamic_update_slice.4
  410.7 0.7 copy-done.6
  411.4 6.0 fusion.1
  417.4 5.9 fusion
  423.3 35.8 %reduce-scatter.5.cloned.1.call-done = bf16[384,192]{0,1:T(8,128)(2,1)} async-done(((bf16[384,6144]{0,1:T(8,128)(2,1)}), bf16[384,192]{0,1:T(8,128)(2,1)}) %reduce-scatter.5.cloned.1.call-update) | async-done | bytes 147472 | tf_op jit(solution)/shard_map/reduce_scatter | solution.py:77
  459.1 1.7 copy.38
  460.9 4.9 all-to-all-start.3
  465.7 0.7 copy.40
  466.5 1.1 fusion.33
  467.6 3.9 all-to-all-done.3
  471.5 0.3 fusion.20
  471.8 0.9 fusion.18
  472.7 763.1 %all-gather.8.cloned.1.call-done = f32[256,6144,8]{1,2,0:T(8,128)} async-done(((f32[1,6144,8]{1,2,0:T(8,128)}), f32[256,6144,8]{1,2,0:T(8,128)}) %all-gather.8.cloned.1.call-update) | async-done | bytes 50331664 | tf_op jit(solution)/shard_map/all_gather | solution.py:125
  1235.8 18.4 %reduce_sum.59 = f32[6144,8]{0,1:T(8,128)} reduce(f32[256,6144,8]{1,2,0:T(8,128)} %all-gather.8.cloned.1.call-done, f32[]{:T(128)} %constant.9.clone.1), dimensions={0}, to_apply=%region_9.0 | reduce | flops 12533760 | bytes 50528260 | tf_op jit(solution)/shard_map/reduce_sum | solution.py:125
  (33 shorter events, 0.2 us)
Async XLA Ops:
  7.2 163.1 %copy-start = (bf16[1,256,6144]{2,1,0:T(8,128)(2,1)S(1)}, bf16[1,256,6144]{2,1,0:T(8,128)(2,1)}, u32[]{:S(2)}) copy-start(bf16[1,256,6144]{2,1,0:T(8,128)(2,1)} %param.12) | copy-start | bytes 9437188
  7.2 91.3 %all-gather.4.cloned.1.call-start = ((), (), s32[]{:S(2)}) async-start(), calls=%async_computation.6 | async-start | bytes 3244032 | tf_op jit(solution)/shard_map/all_gather | solution.py:37
  98.5 4.3 copy-start.3
  102.8 3.6 copy-start.5
  106.4 4.8 copy-start.11
  106.4 59.2 %all-to-all-start = ((bf16[8,48,6144]{2,1,0:T(8,128)(2,1)}), bf16[8,48,6144]{2,1,0:T(8,128)(2,1)}, u32[]{:S(2)}, u32[]{:S(2)}) async-start(bf16[8,48,6144]{2,1,0:T(8,128)(2,1)} %bitcast.61), calls=%async_computation | async-start | bytes 9437184 | tf_op jit(solution)/shard_map/all_to_all | solution.py:45
  111.2 85.0 %all-gather.6.cloned.1.call-start = ((), (), s32[]{:S(2)}) async-start(), calls=%async_computation.8 | async-start | bytes 3244032 | tf_op jit(solution)/shard_map/all_gather | solution.py:38
  112.0 213.9 %reduce-scatter.3.cloned.1.call-start = ((), (), s32[]{:S(2)}) async-start(), calls=%async_computation.7 | async-start | bytes 4866048 | tf_op jit(solution)/shard_map/reduce_scatter | solution.py:74
  174.4 284.8 %reduce-scatter.5.cloned.1.call-start = ((), (), s32[]{:S(2)}) async-start(), calls=%async_computation.9 | async-start | bytes 4866048 | tf_op jit(solution)/shard_map/reduce_scatter | solution.py:77
  261.2 2.2 copy-start.2
  263.5 2.1 copy-start.4
  264.9 0.7 copy-start.9
  265.6 4.0 copy-start.12
  269.5 69.0 %copy-start.8 = (bf16[192,192]{0,1:T(8,128)(2,1)S(1)}, bf16[192,192]{0,1:T(8,128)(2,1)}, u32[]{:S(2)}) copy-start(bf16[192,192]{0,1:T(8,128)(2,1)} %copy.37) | copy-start | bytes 221188
  269.5 140.6 %copy-start.7 = (bf16[192,192]{1,0:T(8,128)(2,1)S(1)}, bf16[192,192]{1,0:T(8,128)(2,1)}, u32[]{:S(2)}) copy-start(bf16[192,192]{1,0:T(8,128)(2,1)} %param.7) | copy-start | bytes 221188
  327.6 10.6 all-to-all-start.1
  332.5 903.3 %all-gather.8.cloned.1.call-start = ((), (), s32[]{:S(2)}) async-start(), calls=%async_computation.10 | async-start | bytes 50528256 | tf_op jit(solution)/shard_map/all_gather | solution.py:125
  410.7 0.7 copy-start.6
  411.4 6.0 copy-start.10
  460.9 10.7 all-to-all-start.3
  1235.8 18.4 %copy-start.1 = (bf16[1,256,6144]{2,1,0:T(8,128)(2,1)S(1)}, bf16[1,256,6144]{2,1,0:T(8,128)(2,1)}, u32[]{:S(2)}) copy-start(bf16[1,256,6144]{2,1,0:T(8,128)(2,1)} %param.12) | copy-start | bytes 9437188
Sparse Core Ops, SparseCore 0:
  11.3 87.0 all-gather.3
  115.3 80.7 all-gather.5
  200.4 125.4 reduce-scatter.2
  330.0 129.0 reduce-scatter.4
  460.8 774.8 all-gather.7
